TPU v7x, 256 devices: a whole 4x4x8 slice. The times are simulated.
256 devices in a mesh: dp: 4 (over x), rows: 64 (over y, z, core).
Axes of the slice: x: 4, y: 4, z: 8, core: 2. Of those that a mesh axis runs over, the one named last changes fastest.
Arguments:
- grads: bfloat16 [4, 64, 1024, 1024], P('dp', None, 'rows'), may hold values from -6 to 6
- weight: bfloat16 [64, 1024, 1024], P(None, 'rows'), may hold values from -6 to 6
- basis: float32 [64, 1024, 256], P(None, 'rows'), may hold values from -6 to 6
- first_moment: float32 [256, 256, 1024], P('rows', None, 'dp'), may hold values from -6 to 6
- second_moment: float32 [256, 256, 1024], P('rows', None, 'dp'), may hold values from 0.5 to 4
- sketch: bfloat16 [1024, 256], replicated, may hold values from -6 to 6
- owner: int32 [64], replicated, may hold values from 0 to 63, as said below
- rank: int32 [64], replicated, may hold values from 128 to 256
Outputs:
- new_weight: bfloat16 [64, 1024, 1024], P(None, 'rows')
- new_basis: float32 [64, 1024, 256], P(None, 'rows')
- first_out: float32 [256, 256, 1024], P('rows', None, 'dp')
- second_out: float32 [256, 256, 1024], P('rows', None, 'dp')
Inputs may be any that keep to these rules, and one draw needn't show every extreme that they name: No owner is named by more than 4 matrices, and some owner is named by exactly 4.
All inputs are finite; a program needn't handle non-finite values.
Results may differ from a plain program's by a relative error of at most 0.012.
Values may be sent and summed in bfloat16 or wider, within the bound.
A program may use at most 128 MiB of HBM per device.

v0:
```python
import jax
import jax.numpy as jnp
from jax import lax
from jax.sharding import PartitionSpec as P

beta_one = 0.9
beta_two = 0.95
bias_one = 1.0 - 0.9**10
bias_two = 1.0 - 0.95**10
step_size = 0.5
epsilon = 1e-08


def slot_of(owner, capacity):
    same = owner[:, None] == owner[None, :]
    places = jnp.arange(owner.shape[0], dtype=jnp.int32)
    earlier = places[None, :] < places[:, None]
    within = jnp.sum((same & earlier).astype(jnp.int32), axis=1)
    return owner * capacity + within


def spread_half(placing, data, capacity, owners):
    flat = data.reshape(data.shape[0], -1)
    moved = jnp.dot(placing.T, flat, preferred_element_type=jnp.float32).astype(jnp.bfloat16)
    return moved.reshape(capacity, owners, data.shape[1], data.shape[2])


def spread_full(placing, data, capacity, owners):
    flat = data.reshape(data.shape[0], -1)
    moved = jnp.dot(placing.T, flat, precision=lax.Precision.HIGHEST)
    return moved.reshape(capacity, owners, data.shape[1], data.shape[2])


def collect_half(placing, data):
    flat = data.reshape(placing.shape[1], -1)
    picked = jnp.dot(placing, flat, preferred_element_type=jnp.float32).astype(jnp.bfloat16)
    return picked.reshape(placing.shape[0], data.shape[2], data.shape[3])


def collect_full(placing, data):
    flat = data.reshape(placing.shape[1], -1)
    picked = jnp.dot(placing, flat, precision=lax.Precision.HIGHEST)
    return picked.reshape(placing.shape[0], data.shape[2], data.shape[3])


def per_device(grads, weight, basis, first_moment, second_moment, sketch, owner, rank):
    owners = lax.axis_size("rows")
    here = lax.axis_index("rows")
    group = lax.axis_index("dp")
    capacity = first_moment.shape[0]
    rank_full = first_moment.shape[1]
    quarter = first_moment.shape[2]
    shard = weight.shape[1]
    width = weight.shape[2]
    total_rows = shard * owners
    root = float(total_rows) ** 0.5
    inverse_root = float(total_rows) ** (-0.5)
    slots = slot_of(owner, capacity)
    column = slots % capacity * owners + slots // capacity
    placing = column[:, None] == jnp.arange(capacity * owners, dtype=jnp.int32)[None, :]
    place_half = placing.astype(jnp.bfloat16)
    place_full = placing.astype(jnp.float32)
    sent_basis = lax.all_to_all(
        spread_full(place_full, basis, capacity, owners),
        "rows",
        split_axis=1,
        concat_axis=1,
        tiled=True,
    )
    old_basis = sent_basis.reshape(capacity, total_rows, rank_full)
    total = lax.psum(grads[0], "dp").astype(jnp.float32).astype(jnp.bfloat16)
    sent_grad = lax.all_to_all(
        spread_half(place_half, total, capacity, owners),
        "rows",
        split_axis=1,
        concat_axis=1,
        tiled=True,
    )
    whole = sent_grad.reshape(capacity, total_rows, width)
    own = lax.dynamic_slice_in_dim(whole, group * quarter, quarter, 2)
    sample = jnp.einsum("cmd,dr->cmr", whole, sketch, preferred_element_type=jnp.float32)
    matched = slots[:, None] == (here * capacity + jnp.arange(capacity, dtype=jnp.int32))[None, :]
    valid = jnp.any(matched, axis=0).astype(jnp.float32)
    rank_slot = jnp.sum(jnp.where(matched, rank[:, None], 0), axis=0)
    projected = (
        jnp.einsum(
            "cmr,cmd->crd", old_basis, own.astype(jnp.float32), precision=lax.Precision.HIGHEST
        )
        * inverse_root
    )
    first_new = beta_one * first_moment + (1.0 - beta_one) * projected
    second_new = beta_two * second_moment + (1.0 - beta_two) * projected * projected
    keeping = (jnp.arange(rank_full, dtype=jnp.int32)[None, :] < rank_slot[:, None]).astype(
        jnp.float32
    )[:, :, None]
    update = keeping * (first_new / bias_one) / (jnp.sqrt(second_new / bias_two) + epsilon)
    delta = (
        jnp.einsum("cmr,crd->cmd", old_basis, update, precision=lax.Precision.HIGHEST)
        * inverse_root
    ).astype(jnp.bfloat16)
    gram = jnp.einsum("cmr,cms->crs", sample, sample, precision=lax.Precision.HIGHEST)
    gram = gram + (1.0 - valid)[:, None, None] * jnp.eye(rank_full, dtype=jnp.float32)[None, :, :]
    lower = jnp.linalg.cholesky(gram)
    new_basis = (
        lax.linalg.triangular_solve(lower, sample, left_side=False, lower=True, transpose_a=True)
        * root
    )
    back_delta = lax.all_to_all(
        delta.reshape(capacity, owners, shard, quarter),
        "rows",
        split_axis=1,
        concat_axis=1,
        tiled=True,
    )
    full_delta = lax.all_gather(collect_half(place_half, back_delta), "dp", axis=2, tiled=True)
    back_basis = lax.all_to_all(
        new_basis.reshape(capacity, owners, shard, rank_full),
        "rows",
        split_axis=1,
        concat_axis=1,
        tiled=True,
    )
    mine_basis = collect_full(place_full, back_basis)
    new_weight = (weight.astype(jnp.float32) - step_size * full_delta.astype(jnp.float32)).astype(
        jnp.bfloat16
    )
    scale_slot = valid[:, None, None]
    return (new_weight, mine_basis, first_new * scale_slot, second_new * scale_slot)


def solution(mesh):
    in_specs = (
        P("dp", None, "rows", None),
        P(None, "rows", None),
        P(None, "rows", None),
        P("rows", None, "dp"),
        P("rows", None, "dp"),
        P(),
        P(),
        P(),
    )
    out_specs = (
        P(None, "rows", None),
        P(None, "rows", None),
        P("rows", None, "dp"),
        P("rows", None, "dp"),
    )
    return jax.shard_map(
        per_device, mesh=mesh, in_specs=in_specs, out_specs=out_specs, check_vma=False
    )
```

profile of v0, /device:TPU:1, one launch (start us, length us, event | category | flops | bytes accessed | tf_op | source)
XLA Modules:
  0.0 740.5 jit_solution(191552147987780826)
XLA Ops:
  16.7 13.5 %all-to-all-start = ((f32[4,64,16,256]{3,2,0,1:T(8,128)}), f32[4,64,16,256]{3,2,0,1:T(8,128)}, u32[]{:S(2)}, u32[]{:S(2)}) async-start(f32[4,64,16,256]{3,2,0,1:T(8,128)} %copy.72), calls=%async_computation | async-start | bytes 8388608 | tf_op jit(solution)/shard_map/all_to_all | solution.py:63
  33.1 65.7 %all-reduce.3.cloned.1.call-done = bf16[64,16384]{1,0:T(8,128)(2,1)} async-done(((bf16[64,16384]{1,0:T(8,128)(2,1)}), bf16[64,16384]{1,0:T(8,128)(2,1)}) %all-reduce.3.cloned.1.call-update) | async-done | bytes 2097168 | tf_op jit(solution)/shard_map/psum | solution.py:71
  98.7 7.3 convolution_convert_fusion
  106.0 15.6 %copy.106 = bf16[32,8,16,1024]{3,2,1,0:T(8,128)(2,1)} copy(bf16[32,8,16,1024]{3,1,2,0:T(8,128)(2,1)} %bitcast.92) | data formatting | bytes 16777216
  121.6 8.5 %copy.74 = bf16[4,64,16,1024]{3,2,0,1:T(8,128)(2,1)} copy(bf16[4,64,16,1024]{3,2,1,0:T(8,128)(2,1)} %bitcast.93) | data formatting | bytes 16777216 | tf_op jit(solution)/shard_map/reshape | solution.py:25
  130.2 11.0 %all-to-all-start.1 = ((bf16[4,64,16,1024]{3,2,0,1:T(8,128)(2,1)}), bf16[4,64,16,1024]{3,2,0,1:T(8,128)(2,1)}, u32[]{:S(2)}, u32[]{:S(2)}) async-start(bf16[4,64,16,1024]{3,2,0,1:T(8,128)(2,1)} %copy.74), calls=%async_computation.1 | async-start | bytes 16777216 | tf_op jit(solution)/shard_map/all_to_all | solution.py:72
  141.8 4.8 copy.73
  146.6 180.4 %all-to-all-done.1 = bf16[4,64,16,1024]{3,2,0,1:T(8,128)(2,1)} async-done(((bf16[4,64,16,1024]{3,2,0,1:T(8,128)(2,1)}), bf16[4,64,16,1024]{3,2,0,1:T(8,128)(2,1)}, u32[]{:S(2)}, u32[]{:S(2)}) %all-to-all-start.1) | async-done | bytes 8388640 | tf_op jit(solution)/shard_map/all_to_all | solution.py:72
  327.0 8.5 %copy.75 = bf16[4,64,16,1024]{3,2,1,0:T(8,128)(2,1)} copy(bf16[4,64,16,1024]{3,2,0,1:T(8,128)(2,1)} %all-to-all-done.1) | data formatting | bytes 16777216 | tf_op jit(solution)/shard_map/all_to_all | solution.py:72
  335.5 7.8 %fusion.14 = f32[4,1024,256]{2,1,0:T(8,128)} fusion(bf16[4,1024,1024]{2,1,0:T(8,128)(2,1)} %bitcast.100, bf16[1024,256]{1,0:T(8,128)(2,1)S(1)} %copy-done), kind=kOutput, calls=%fused_computation.29 | convolution fusion | flops 2147483648 | bytes 13107200 | tf_op jit(solution)/shard_map/cmd,dr->cmr/dot_general | solution.py:81
  343.4 6.8 broadcast_multiply_fusion
  350.2 4.7 multiply_convert_fusion
  356.6 6.4 all-to-all-start.2
  363.0 10.0 %fusion.50 = f32[4,256,256]{2,1,0:T(8,128)S(1)} fusion(f32[4,1024,256]{2,1,0:T(8,128)} %fusion.14), kind=kOutput, calls=%fused_computation.97 | convolution fusion | flops 3221225472 | bytes 5242880 | tf_op jit(solution)/shard_map/cmr,cms->crs/dot_general | solution.py:101
  374.6 46.9 %custom-call.16 = f32[4,128,128]{2,1,0:T(8,128)S(1)} custom-call(f32[4,128,128]{2,1,0:T(8,128)S(1)} %cholesky.122), custom_call_target="Cholesky" | custom-call | tf_op jit(solution)/shard_map/jit(cholesky)/cholesky | solution.py:103
  421.7 39.3 %custom-call.17 = f32[4,1,128,128]{2,3,1,0:T(8,128)S(1)} custom-call(f32[4,1,128,128]{3,2,1,0:T(8,128)S(1)} %select_bitcast_fusion), custom_call_target="InvertDiagBlocksLowerTriangular" | custom-call | tf_op jit(solution)/shard_map/jit(cholesky)/cholesky | solution.py:103
  464.0 47.1 %custom-call.18 = f32[4,128,128]{2,1,0:T(8,128)S(1)} custom-call(f32[4,128,128]{2,1,0:T(8,128)S(1)} %convolution_subtract_fusion), custom_call_target="Cholesky" | custom-call | tf_op jit(solution)/shard_map/jit(cholesky)/cholesky | solution.py:103
  511.7 5.3 while.1
  517.0 79.4 %custom-call.19 = f32[4,2,128,128]{2,3,1,0:T(8,128)S(1)} custom-call(f32[4,2,128,128]{3,2,1,0:T(8,128)} %bitcast.111), custom_call_target="InvertDiagBlocksLowerTriangular" | custom-call | tf_op jit(solution)/shard_map/triangular_solve | solution.py:105
  606.5 10.5 %all-to-all-start.3 = ((f32[4,64,16,256]{3,2,0,1:T(8,128)}), f32[4,64,16,256]{3,2,0,1:T(8,128)}, u32[]{:S(2)}, u32[]{:S(2)}) async-start(f32[4,64,16,256]{3,2,0,1:T(8,128)} %copy_multiply_fusion), calls=%async_computation.3 | async-start | bytes 8388608 | tf_op jit(solution)/shard_map/all_to_all | solution.py:116
  621.6 35.8 %all-gather.2.cloned.1.call-done = bf16[64,16,1024]{2,1,0:T(8,128)(2,1)} async-done(((bf16[64,16,256]{2,1,0:T(8,128)(2,1)}), bf16[64,16,1024]{2,1,0:T(8,128)(2,1)}) %all-gather.2.cloned.1.call-update) | async-done | bytes 2097168 | tf_op jit(solution)/shard_map/all_gather | solution.py:115
  661.2 51.7 %all-to-all-done.3 = f32[4,64,16,256]{3,2,0,1:T(8,128)} async-done(((f32[4,64,16,256]{3,2,0,1:T(8,128)}), f32[4,64,16,256]{3,2,0,1:T(8,128)}, u32[]{:S(2)}, u32[]{:S(2)}) %all-to-all-start.3) | async-done | bytes 4194336 | tf_op jit(solution)/shard_map/all_to_all | solution.py:116
  715.7 5.7 copy.109
  721.5 5.7 copy.89
  (76 shorter events, 52.4 us)
Async XLA Ops:
  7.2 328.4 %copy-start = (bf16[1024,256]{1,0:T(8,128)(2,1)S(1)}, bf16[1024,256]{1,0:T(8,128)(2,1)}, u32[]{:S(2)}) copy-start(bf16[1024,256]{1,0:T(8,128)(2,1)} %param.13) | copy-start | bytes 1572868
  16.7 13.8 %copy-start.6 = (bf16[1,64,16,1024]{3,2,1,0:T(8,128)(2,1)S(1)}, bf16[1,64,16,1024]{3,2,1,0:T(8,128)(2,1)}, u32[]{:S(2)}) copy-start(bf16[1,64,16,1024]{3,2,1,0:T(8,128)(2,1)} %param.8) | copy-start | bytes 6291460
  16.7 113.5 %all-to-all-start = ((f32[4,64,16,256]{3,2,0,1:T(8,128)}), f32[4,64,16,256]{3,2,0,1:T(8,128)}, u32[]{:S(2)}, u32[]{:S(2)}) async-start(f32[4,64,16,256]{3,2,0,1:T(8,128)} %copy.72), calls=%async_computation | async-start | bytes 8388608 | tf_op jit(solution)/shard_map/all_to_all | solution.py:63
  30.2 68.6 %all-reduce.3.cloned.1.call-start = ((), (), s32[]{:S(2)}) async-start(), calls=%async_computation.4 | async-start | bytes 4194304 | tf_op jit(solution)/shard_map/psum | solution.py:71
  130.2 11.3 %copy-start.9 = (s32[64]{0:T(128)S(1)}, s32[64]{0:T(128)}, u32[]{:S(2)}) copy-start(s32[64]{0:T(128)} %param.15) | copy-start | bytes 772
  130.2 196.8 %all-to-all-start.1 = ((bf16[4,64,16,1024]{3,2,0,1:T(8,128)(2,1)}), bf16[4,64,16,1024]{3,2,0,1:T(8,128)(2,1)}, u32[]{:S(2)}, u32[]{:S(2)}) async-start(bf16[4,64,16,1024]{3,2,0,1:T(8,128)(2,1)} %copy.74), calls=%async_computation.1 | async-start | bytes 16777216 | tf_op jit(solution)/shard_map/all_to_all | solution.py:72
  335.5 7.9 %copy-start.3 = (f32[4,64,16,256]{3,2,1,0:T(8,128)S(1)}, f32[4,64,16,256]{3,2,1,0:T(8,128)}, u32[]{:S(2)}) copy-start(f32[4,64,16,256]{3,2,1,0:T(8,128)} %copy.73) | copy-start | bytes 12582916
  335.5 7.9 %copy-start.7 = (f32[4,256,256]{2,1,0:T(8,128)S(1)}, f32[4,256,256]{2,1,0:T(8,128)}, u32[]{:S(2)}) copy-start(f32[4,256,256]{2,1,0:T(8,128)} %param.12) | copy-start | bytes 3145732
  335.5 7.9 %copy-start.8 = (f32[4,256,256]{2,1,0:T(8,128)S(1)}, f32[4,256,256]{2,1,0:T(8,128)}, u32[]{:S(2)}) copy-start(f32[4,256,256]{2,1,0:T(8,128)} %param.11) | copy-start | bytes 3145732
  356.6 250.0 %all-to-all-start.2 = ((bf16[4,64,16,256]{3,2,0,1:T(8,128)(2,1)}), bf16[4,64,16,256]{3,2,0,1:T(8,128)(2,1)}, u32[]{:S(2)}, u32[]{:S(2)}) async-start(bf16[4,64,16,256]{3,2,0,1:T(8,128)(2,1)} %copy.77), calls=%async_computation.2 | async-start | bytes 4194304 | tf_op jit(solution)/shard_map/all_to_all | solution.py:108
  373.6 1.0 copy-start.4
  596.4 5.6 copy-start.2
  606.5 106.4 %all-to-all-start.3 = ((f32[4,64,16,256]{3,2,0,1:T(8,128)}), f32[4,64,16,256]{3,2,0,1:T(8,128)}, u32[]{:S(2)}, u32[]{:S(2)}) async-start(f32[4,64,16,256]{3,2,0,1:T(8,128)} %copy_multiply_fusion), calls=%async_computation.3 | async-start | bytes 8388608 | tf_op jit(solution)/shard_map/all_to_all | solution.py:116
  617.1 40.3 %all-gather.2.cloned.1.call-start = ((), (), s32[]{:S(2)}) async-start(), calls=%async_computation.5 | async-start | bytes 2621440 | tf_op jit(solution)/shard_map/all_gather | solution.py:115
  619.1 38.2 %copy-start.5 = (bf16[64,16,1024]{2,1,0:T(8,128)(2,1)S(1)}, bf16[64,16,1024]{2,1,0:T(8,128)(2,1)}, u32[]{:S(2)}) copy-start(bf16[64,16,1024]{2,1,0:T(8,128)(2,1)} %param.9) | copy-start | bytes 6291460
  721.5 11.7 %copy-start.1 = (bf16[1024,256]{1,0:T(8,128)(2,1)S(1)}, bf16[1024,256]{1,0:T(8,128)(2,1)}, u32[]{:S(2)}) copy-start(bf16[1024,256]{1,0:T(8,128)(2,1)} %param.13) | copy-start | bytes 1572868
Sparse Core Ops, SparseCore 0:
  33.9 64.7 all-reduce.2
  621.7 35.6 all-gather.1
where the time goes:
time: 746 us; the launch traced here: 740 us
  waiting for transfers between devices  334 us (45%)
  other arithmetic  222 us (30%)
  local copies, waits for them, and re-layouts  72.4 us (10%)
  matrix products  55.7 us (7%)
  starting transfers between devices  42 us (6%)
  between operations  14.8 us (2%)
    all_to_all x1, waiting for transfers between devices, per_device(): lax.all_to_all(spread_half(place_half, total, capacity, owners), 'rows',...  180 us
    another operation x10, other arithmetic, per_device(): lower = jnp.linalg.cholesky(gram)  134 us
    another operation x4, other arithmetic, per_device(): lax.linalg.triangular_solve(lower, sample, left_side=False, lower=True, t...  79.6 us
    psum x1, waiting for transfers between devices, per_device(): total = lax.psum(grads[0], 'dp').astype(jnp.float32).astype(jnp.bfloat16)  65.7 us
    all_to_all x1, waiting for transfers between devices, per_device(): lax.all_to_all(new_basis.reshape(capacity, owners, shard, rank_full), 'ro...  51.7 us
    all_gather x1, waiting for transfers between devices, per_device(): lax.all_gather(collect_half(place_half, back_delta), 'dp', axis=2, tiled=...  35.8 us
    unnamed x26, local copies, waits for them, and re-layouts  28.4 us
  transfers between devices with their start and end apart: 6, of which 4 were waited for; matrix products, arithmetic and copies ran while one was open for 39% of the time, Pallas kernels for 0%

commit v1 on v0

--- a/solution.py
+++ b/solution.py
@@ -113,13 +113,10 @@
         tiled=True,
     )
     full_delta = lax.all_gather(collect_half(place_half, back_delta), "dp", axis=2, tiled=True)
-    back_basis = lax.all_to_all(
-        new_basis.reshape(capacity, owners, shard, rank_full),
-        "rows",
-        split_axis=1,
-        concat_axis=1,
-        tiled=True,
-    )
+    own_2 = new_basis.reshape(capacity, owners, shard, rank_full)
+    shards = jnp.split(own_2, lax.axis_size("rows"), axis=1)
+    got = lax.all_to_all(jnp.stack(shards), "rows", 0, 0)
+    back_basis = jnp.concatenate(got, axis=1)
     mine_basis = collect_full(place_full, back_basis)
     new_weight = (weight.astype(jnp.float32) - step_size * full_delta.astype(jnp.float32)).astype(
         jnp.bfloat16

time: 746 us -> 817 us (1.095)
  local copies, waits for them, and re-layouts: 72.4 us -> 129 us
  waiting for transfers between devices: 334 us -> 359 us
    unnamed x26 -> x93, local copies, waits for them, and re-layouts: 28.4 us -> 84.9 us
    all_to_all x1, waiting for transfers between devices: 0.01 us -> 23.4 us  [per_device(): lax.all_to_all(delta.reshape(capacity, owners, shard, quarter), 'rows', s...]
  transfers between devices with their start and end apart: 6 -> 6, of which waited for: 4 -> 5; matrix products, arithmetic and copies ran while one was open for 39% -> 9% of each run, Pallas kernels for 0% -> 0%
where the time goes in v1:
time: 817 us; the launch traced here: 810 us
  waiting for transfers between devices  359 us (44%)
  other arithmetic  220 us (27%)
  local copies, waits for them, and re-layouts  129 us (16%)
  matrix products  51.1 us (6%)
  starting transfers between devices  36.8 us (5%)
  between operations  14.6 us (2%)
    all_to_all x1, waiting for transfers between devices, per_device(): lax.all_to_all(spread_half(place_half, total, capacity, owners), 'rows',...  180 us
    another operation x10, other arithmetic, per_device(): lower = jnp.linalg.cholesky(gram)  134 us
    unnamed x93, local copies, waits for them, and re-layouts  84.9 us
    another operation x4, other arithmetic, per_device(): lax.linalg.triangular_solve(lower, sample, left_side=False, lower=True, t...  79.9 us
    psum x1, waiting for transfers between devices, per_device(): total = lax.psum(grads[0], 'dp').astype(jnp.float32).astype(jnp.bfloat16)  65.6 us
    all_to_all x1, waiting for transfers between devices, per_device(): got = lax.all_to_all(jnp.stack(shards), 'rows', 0, 0)  53 us
    all_gather x1, waiting for transfers between devices, per_device(): lax.all_gather(collect_half(place_half, back_delta), 'dp', axis=2, tiled=...  36.3 us
    all_to_all x1, waiting for transfers between devices, per_device(): lax.all_to_all(delta.reshape(capacity, owners, shard, quarter), 'rows', s...  23.4 us
  transfers between devices with their start and end apart: 6, of which 5 were waited for; matrix products, arithmetic and copies ran while one was open for 9% of the time, Pallas kernels for 0%

profile of v1, /device:TPU:1, one launch (start us, length us, event | category | flops | bytes accessed | tf_op | source)
XLA Modules:
  0.0 810.5 jit_solution(14895756576859859116)
XLA Ops:
  16.6 13.5 %all-to-all-start = ((f32[4,64,16,256]{3,2,0,1:T(8,128)}), f32[4,64,16,256]{3,2,0,1:T(8,128)}, u32[]{:S(2)}, u32[]{:S(2)}) async-start(f32[4,64,16,256]{3,2,0,1:T(8,128)} %copy.201), calls=%async_computation | async-start | bytes 8388608 | tf_op jit(solution)/shard_map/all_to_all | solution.py:63
  33.1 65.6 %all-reduce.3.cloned.1.call-done = bf16[64,16384]{1,0:T(8,128)(2,1)} async-done(((bf16[64,16384]{1,0:T(8,128)(2,1)}), bf16[64,16384]{1,0:T(8,128)(2,1)}) %all-reduce.3.cloned.1.call-update) | async-done | bytes 2097168 | tf_op jit(solution)/shard_map/psum | solution.py:71
  98.7 7.3 convolution_convert_fusion
  105.9 15.8 %copy.235 = bf16[32,8,16,1024]{3,2,1,0:T(8,128)(2,1)} copy(bf16[32,8,16,1024]{3,1,2,0:T(8,128)(2,1)} %bitcast.350) | data formatting | bytes 16777216
  121.7 8.5 %copy.203 = bf16[4,64,16,1024]{3,2,0,1:T(8,128)(2,1)} copy(bf16[4,64,16,1024]{3,2,1,0:T(8,128)(2,1)} %bitcast.351) | data formatting | bytes 16777216 | tf_op jit(solution)/shard_map/reshape | solution.py:25
  130.2 11.0 %all-to-all-start.1 = ((bf16[4,64,16,1024]{3,2,0,1:T(8,128)(2,1)}), bf16[4,64,16,1024]{3,2,0,1:T(8,128)(2,1)}, u32[]{:S(2)}, u32[]{:S(2)}) async-start(bf16[4,64,16,1024]{3,2,0,1:T(8,128)(2,1)} %copy.203), calls=%async_computation.1 | async-start | bytes 16777216 | tf_op jit(solution)/shard_map/all_to_all | solution.py:72
  146.6 180.4 %all-to-all-done.1 = bf16[4,64,16,1024]{3,2,0,1:T(8,128)(2,1)} async-done(((bf16[4,64,16,1024]{3,2,0,1:T(8,128)(2,1)}), bf16[4,64,16,1024]{3,2,0,1:T(8,128)(2,1)}, u32[]{:S(2)}, u32[]{:S(2)}) %all-to-all-start.1) | async-done | bytes 8388640 | tf_op jit(solution)/shard_map/all_to_all | solution.py:72
  327.0 8.5 %copy.204 = bf16[4,64,16,1024]{3,2,1,0:T(8,128)(2,1)} copy(bf16[4,64,16,1024]{3,2,0,1:T(8,128)(2,1)} %all-to-all-done.1) | data formatting | bytes 16777216 | tf_op jit(solution)/shard_map/all_to_all | solution.py:72
  335.6 5.8 fusion.14
  343.4 7.1 fusion.50
  352.1 47.1 %custom-call.16 = f32[4,128,128]{2,1,0:T(8,128)S(1)} custom-call(f32[4,128,128]{2,1,0:T(8,128)S(1)} %cholesky.122), custom_call_target="Cholesky" | custom-call | tf_op jit(solution)/shard_map/jit(cholesky)/cholesky | solution.py:103
  399.3 39.3 %custom-call.17 = f32[4,1,128,128]{2,3,1,0:T(8,128)S(1)} custom-call(f32[4,1,128,128]{3,2,1,0:T(8,128)S(1)} %select_bitcast_fusion), custom_call_target="InvertDiagBlocksLowerTriangular" | custom-call | tf_op jit(solution)/shard_map/jit(cholesky)/cholesky | solution.py:103
  441.6 46.9 %custom-call.18 = f32[4,128,128]{2,1,0:T(8,128)S(1)} custom-call(f32[4,128,128]{2,1,0:T(8,128)S(1)} %convolution_subtract_fusion), custom_call_target="Cholesky" | custom-call | tf_op jit(solution)/shard_map/jit(cholesky)/cholesky | solution.py:103
  489.1 5.5 while.1
  494.5 79.6 %custom-call.19 = f32[4,2,128,128]{2,3,1,0:T(8,128)S(1)} custom-call(f32[4,2,128,128]{3,2,1,0:T(8,128)} %bitcast.369), custom_call_target="InvertDiagBlocksLowerTriangular" | custom-call | tf_op jit(solution)/shard_map/triangular_solve | solution.py:105
  610.5 6.8 broadcast_multiply_fusion
  617.3 5.1 multiply_convert_fusion
  624.0 5.9 all-to-all-start.2
  657.8 23.4 %all-to-all-done.2 = bf16[4,64,16,256]{3,2,0,1:T(8,128)(2,1)S(1)} async-done(((bf16[4,64,16,256]{3,2,0,1:T(8,128)(2,1)}), bf16[4,64,16,256]{3,2,0,1:T(8,128)(2,1)S(1)}, u32[]{:S(2)}, u32[]{:S(2)}) %all-to-all-start.2) | async-done | bytes 2097184 | tf_op jit(solution)/shard_map/all_to_all | solution.py:108
  681.2 6.0 all-to-all-start.3
  689.9 36.3 %all-gather.2.cloned.1.call-done = bf16[64,16,1024]{2,1,0:T(8,128)(2,1)} async-done(((bf16[64,16,256]{2,1,0:T(8,128)(2,1)}), bf16[64,16,1024]{2,1,0:T(8,128)(2,1)}) %all-gather.2.cloned.1.call-update) | async-done | bytes 2097168 | tf_op jit(solution)/shard_map/all_gather | solution.py:115
  730.1 53.0 %all-to-all-done.3 = f32[64,4,1,16,256]{4,3,1,2,0:T(8,128)} async-done(((f32[64,4,1,16,256]{4,3,1,2,0:T(8,128)}), f32[64,4,1,16,256]{4,3,1,2,0:T(8,128)}, u32[]{:S(2)}, u32[]{:S(2)}) %all-to-all-start.3) | async-done | bytes 4194336 | tf_op jit(solution)/shard_map/all_to_all | solution.py:118
  785.9 5.7 copy.238
  791.6 5.8 copy.218
  (144 shorter events, 111.3 us)
Async XLA Ops:
  7.2 328.4 %copy-start = (bf16[1024,256]{1,0:T(8,128)(2,1)S(1)}, bf16[1024,256]{1,0:T(8,128)(2,1)}, u32[]{:S(2)}) copy-start(bf16[1024,256]{1,0:T(8,128)(2,1)} %param.13) | copy-start | bytes 1572868
  16.6 13.9 %copy-start.8 = (bf16[1,64,16,1024]{3,2,1,0:T(8,128)(2,1)S(1)}, bf16[1,64,16,1024]{3,2,1,0:T(8,128)(2,1)}, u32[]{:S(2)}) copy-start(bf16[1,64,16,1024]{3,2,1,0:T(8,128)(2,1)} %param.8) | copy-start | bytes 6291460
  16.6 113.6 %all-to-all-start = ((f32[4,64,16,256]{3,2,0,1:T(8,128)}), f32[4,64,16,256]{3,2,0,1:T(8,128)}, u32[]{:S(2)}, u32[]{:S(2)}) async-start(f32[4,64,16,256]{3,2,0,1:T(8,128)} %copy.201), calls=%async_computation | async-start | bytes 8388608 | tf_op jit(solution)/shard_map/all_to_all | solution.py:63
  30.1 68.6 %all-reduce.3.cloned.1.call-start = ((), (), s32[]{:S(2)}) async-start(), calls=%async_computation.4 | async-start | bytes 4194304 | tf_op jit(solution)/shard_map/psum | solution.py:71
  130.2 11.3 %copy-start.11 = (s32[64]{0:T(128)S(1)}, s32[64]{0:T(128)}, u32[]{:S(2)}) copy-start(s32[64]{0:T(128)} %param.15) | copy-start | bytes 772
  130.2 196.8 %all-to-all-start.1 = ((bf16[4,64,16,1024]{3,2,0,1:T(8,128)(2,1)}), bf16[4,64,16,1024]{3,2,0,1:T(8,128)(2,1)}, u32[]{:S(2)}, u32[]{:S(2)}) async-start(bf16[4,64,16,1024]{3,2,0,1:T(8,128)(2,1)} %copy.203), calls=%async_computation.1 | async-start | bytes 16777216 | tf_op jit(solution)/shard_map/all_to_all | solution.py:72
  341.4 2.0 copy-start.2
  351.1 1.0 copy-start.6
  574.2 5.6 copy-start.3
  581.8 28.6 %copy-start.10 = (f32[4,256,256]{2,1,0:T(8,128)S(1)}, f32[4,256,256]{2,1,0:T(8,128)}, u32[]{:S(2)}) copy-start(f32[4,256,256]{2,1,0:T(8,128)} %param.11) | copy-start | bytes 3145732
  582.3 35.0 %copy-start.5 = (f32[4,64,16,256]{3,2,0,1:T(8,128)}, f32[4,64,16,256]{3,2,0,1:T(8,128)S(1)}, u32[]{:S(2)}) copy-start(f32[4,64,16,256]{3,2,0,1:T(8,128)S(1)} %copy_multiply_fusion) | copy-start | bytes 12582916
  582.3 28.1 %copy-start.4 = (f32[4,64,16,256]{3,2,1,0:T(8,128)S(1)}, f32[4,64,16,256]{3,2,1,0:T(8,128)}, u32[]{:S(2)}) copy-start(f32[4,64,16,256]{3,2,1,0:T(8,128)} %copy.202) | copy-start | bytes 12582916
  582.3 28.1 %copy-start.9 = (f32[4,256,256]{2,1,0:T(8,128)S(1)}, f32[4,256,256]{2,1,0:T(8,128)}, u32[]{:S(2)}) copy-start(f32[4,256,256]{2,1,0:T(8,128)} %param.12) | copy-start | bytes 3145732
  624.0 57.2 %all-to-all-start.2 = ((bf16[4,64,16,256]{3,2,0,1:T(8,128)(2,1)}), bf16[4,64,16,256]{3,2,0,1:T(8,128)(2,1)S(1)}, u32[]{:S(2)}, u32[]{:S(2)}) async-start(bf16[4,64,16,256]{3,2,0,1:T(8,128)(2,1)} %copy.206), calls=%async_computation.2 | async-start | bytes 4194304 | tf_op jit(solution)/shard_map/all_to_all | solution.py:108
  681.2 101.9 %all-to-all-start.3 = ((f32[64,4,1,16,256]{4,3,1,2,0:T(8,128)}), f32[64,4,1,16,256]{4,3,1,2,0:T(8,128)}, u32[]{:S(2)}, u32[]{:S(2)}) async-start(f32[64,4,1,16,256]{4,3,1,2,0:T(8,128)} %constant_dynamic-update-slice_fusion), calls=%async_computation.3 | async-start | bytes 8388608 | tf_op jit(solution)/shard_map/all_to_all | solution.py:118
  687.2 39.0 %all-gather.2.cloned.1.call-start = ((), (), s32[]{:S(2)}) async-start(), calls=%async_computation.5 | async-start | bytes 2621440 | tf_op jit(solution)/shard_map/all_gather | solution.py:115
  687.5 38.8 %copy-start.7 = (bf16[64,16,1024]{2,1,0:T(8,128)(2,1)S(1)}, bf16[64,16,1024]{2,1,0:T(8,128)(2,1)}, u32[]{:S(2)}) copy-start(bf16[64,16,1024]{2,1,0:T(8,128)(2,1)} %param.9) | copy-start | bytes 6291460
  791.6 11.8 %copy-start.1 = (bf16[1024,256]{1,0:T(8,128)(2,1)S(1)}, bf16[1024,256]{1,0:T(8,128)(2,1)}, u32[]{:S(2)}) copy-start(bf16[1024,256]{1,0:T(8,128)(2,1)} %param.13) | copy-start | bytes 1572868
Sparse Core Ops, SparseCore 0:
  33.9 64.7 all-reduce.2
  690.6 35.6 all-gather.1
